TPU v7x, 128 devices: a whole 4x4x4 slice. The times are simulated.
128 devices in a mesh: rows: 8 (over y, x_hi), cols: 16 (over x_lo, z, core).
Axes of the slice: x: 4 (x_hi: 2, x_lo: 2; x = x_hi * 2 + x_lo), y: 4, z: 4, core: 2. Of those that a mesh axis runs over, the one named last changes fastest.
Arguments:
- object_field: float32 [2, 2048, 4096], P(None, 'rows', 'cols'), may hold values from -6 to 6
- probe: float32 [2, 256, 256], replicated, may hold values from -6 to 6
- positions: int32 [8, 16, 6, 2], P('rows', 'cols'), may hold values from 0 to 256
- counts: int32 [8, 16], P('rows', 'cols'), may hold values from 2 to 6
- intensity: int32 [8, 16, 6, 256, 256], P('rows', 'cols'), may hold values from 0 to 4000
Outputs:
- updated_field: float32 [2, 2048, 4096], P(None, 'rows', 'cols')
Inputs may be any that keep to these rules, and one draw needn't show every extreme that they name: Only the first counts[a, b] entries of tile (a, b) in positions and intensity are used.
All inputs are finite; a program needn't handle non-finite values.
Results may differ from a plain program's by a relative error of at most 0.00029.
Values sent between devices are 32-bit elements; how exact they have to be, the bound alone decides.
No kernel may reach another device: no remote copies, remote signals or barrier semaphores. Data moves between devices by JAX's collectives and lax.ppermute only.
A program may use at most 64 MiB of HBM per device.

v0:
```python
import functools

import jax
import jax.numpy as jnp
import numpy as np
from jax import lax
from jax.experimental import pallas as pl
from jax.experimental.pallas import tpu as pltpu
from jax.sharding import PartitionSpec as P

MARGIN = 128
HALF = 128


step_rate = 0.02
photon_unit = 0.001


def rotation_tables(length):
    half = length // 2
    index = np.arange(half, dtype=np.int64)
    angle = (index[:, None] * index[None, :] % half) * (2.0 * np.pi / half)
    norm = 1.0 / np.sqrt(length)
    cosine = np.cos(angle) * norm
    sine = np.sin(angle) * norm
    mixed = np.block([[cosine, -sine], [sine, cosine]]).astype(np.float32)
    turn = index * (2.0 * np.pi / length)
    twiddle = np.stack([np.cos(turn), -np.sin(turn)]).astype(np.float32)
    return mixed, twiddle


def split_order(length):
    half = length // 2
    order = np.concatenate([np.arange(half) * 2, np.arange(half) * 2 + 1])
    return (np.arange(length)[:, None] == order[None, :]).astype(np.float32)


def prepare_body(positions, intensity, probe, order, measured, rolled):
    slots = intensity.shape[0]
    size = probe.shape[1]
    half = size // 2
    moves = order[...]

    def one_slot(slot, carry):
        scol = positions[slot, 1]
        shift = lax.rem(scol, size)
        for part in range(2):
            rolled[slot, part] = pltpu.roll(probe[part], shift, 1)
        full = intensity[slot]
        for parity in range(2):
            counts = full.reshape(half, 2, size)[:, parity, :]
            upper = lax.shift_right_logical(counts, 8).astype(jnp.float32).astype(jnp.bfloat16)
            lower = lax.bitwise_and(counts, 255).astype(jnp.float32).astype(jnp.bfloat16)
            moved = 256.0 * jnp.dot(upper, moves, preferred_element_type=jnp.float32)
            moved = moved + jnp.dot(lower, moves, preferred_element_type=jnp.float32)
            measured[slot, parity] = moved * photon_unit
        return carry

    lax.fori_loop(0, slots, one_slot, 0)


def prepare(positions, intensity, probe, order):
    slots, size = intensity.shape[0], probe.shape[1]
    vmem = pl.BlockSpec(memory_space=pltpu.VMEM)
    return pl.pallas_call(
        prepare_body,
        out_shape=(
            jax.ShapeDtypeStruct((slots, 2, size // 2, size), jnp.float32),
            jax.ShapeDtypeStruct((slots, 2, size, size), jnp.float32),
        ),
        in_specs=[pl.BlockSpec(memory_space=pltpu.SMEM), vmem, vmem, vmem],
        out_specs=(vmem, vmem),
        compiler_params=pltpu.CompilerParams(vmem_limit_bytes=32 << 20),
        cost_estimate=pl.CostEstimate(flops=slots * 2**27, bytes_accessed=8 << 20, transcendentals=0),
    )(positions, intensity, probe, order)


def halves(value):
    upper = value.astype(jnp.bfloat16)
    lower = (value - upper.astype(jnp.float32)).astype(jnp.bfloat16)
    return upper, lower


def times_table(value, table):
    upper, lower = halves(value)
    packed = jnp.concatenate([upper, lower, upper], axis=1)
    return jnp.dot(packed, table, preferred_element_type=jnp.float32)


def table_times(table, value):
    upper, lower = halves(value)
    packed = jnp.concatenate([upper, lower, upper], axis=0)
    return jnp.dot(table, packed, preferred_element_type=jnp.float32)


def wide(left, right):
    return jnp.concatenate([left, right], axis=1)


def tall(upper, lower):
    return jnp.concatenate([upper, lower], axis=0)


def gradient_body(
    info, positions, counts, ext, strip_a, strip_b, measured, rolled, fore_lane, fore_row, back_row, back_lane,
    twist_lane, twist_row,    out_a, out_b, inner, sides, outer
):
    size = rolled.shape[2]
    half = size // 2
    odd_col = info[1]
    lanes = lax.broadcasted_iota(jnp.int32, (1, half), 1)
    inner[...] = jnp.zeros_like(inner)
    outer[...] = jnp.zeros_like(outer)
    sides[0] = jnp.where(info[4] == 1, 0.0, jnp.where(odd_col == 1, strip_a[0], strip_b[0]))
    sides[1] = jnp.where(info[5] == 1, 0.0, jnp.where(odd_col == 1, strip_b[1], strip_a[1]))

    def one_slot(slot, carry):
        srow = positions[slot, 0]
        scol = positions[slot, 1]
        rows = pl.ds(srow, size)
        near = [lanes + half * block >= scol for block in range(2)]
        blocks = [
            lambda part: sides[0, part, rows, :],
            lambda part: ext[part, 0, rows, :],
            lambda part: ext[part, 1, rows, :],
            lambda part: sides[1, part, rows, :],
        ]

        def patch(part, block):
            return jnp.where(near[block], blocks[block](part), blocks[block + 2](part))

        def probe(part, block):
            return rolled[slot, part, :, half * block : half * (block + 1)]

        lane_r, lane_i = twist_lane[0], twist_lane[1]
        row_r, row_i = twist_row[0], twist_row[1]
        waves = []
        for block in range(2):
            p_r, p_i = probe(0, block), probe(1, block)
            o_r, o_i = patch(0, block), patch(1, block)
            waves.append((p_r * o_r - p_i * o_i, p_r * o_i + p_i * o_r))
        (r0, i0), (r1, i1) = waves
        even = wide(r0 + r1, i0 + i1)
        d_r, d_i = r0 - r1, i0 - i1
        odd = wide(d_r * lane_r - d_i * lane_i, d_r * lane_i + d_i * lane_r)
        even = times_table(even, fore_lane[...])
        odd = times_table(odd, fore_lane[...])
        halves_r = wide(even[:, :half], odd[:, :half])
        halves_i = wide(even[:, half:], odd[:, half:])
        r0, r1 = halves_r[:half], halves_r[half:]
        i0, i1 = halves_i[:half], halves_i[half:]
        even = tall(r0 + r1, i0 + i1)
        d_r, d_i = r0 - r1, i0 - i1
        odd = tall(d_r * row_r - d_i * row_i, d_r * row_i + d_i * row_r)
        spectra = [table_times(fore_row[...], even), table_times(fore_row[...], odd)]
        scaled = []
        for parity, spectrum in enumerate(spectra):
            s_r, s_i = spectrum[:half], spectrum[half:]
            misfit = s_r * s_r + s_i * s_i - measured[slot, parity]
            scaled.append(tall(misfit * s_r, misfit * s_i))
        even = table_times(back_row[...], scaled[0])
        odd = table_times(back_row[...], scaled[1])
        e_r, e_i = even[:half], even[half:]
        o_r, o_i = odd[:half], odd[half:]
        t_r = o_r * row_r + o_i * row_i
        t_i = o_i * row_r - o_r * row_i
        full_r = tall(e_r + t_r, e_r - t_r)
        full_i = tall(e_i + t_i, e_i - t_i)
        even = times_table(wide(full_r[:, :half], full_i[:, :half]), back_lane[...])
        odd = times_table(wide(full_r[:, half:], full_i[:, half:]), back_lane[...])
        e_r, e_i = even[:, :half], even[:, half:]
        o_r, o_i = odd[:, :half], odd[:, half:]
        t_r = o_r * lane_r + o_i * lane_i
        t_i = o_i * lane_r - o_r * lane_i
        outs = [(e_r + t_r, e_i + t_i), (e_r - t_r, e_i - t_i)]
        for block, (b_r, b_i) in enumerate(outs):
            p_r, p_i = probe(0, block), probe(1, block)
            terms = (p_r * b_r + p_i * b_i, p_r * b_i - p_i * b_r)
            for part, term in enumerate(terms):
                low = jnp.where(near[block], term, 0.0)
                high = jnp.where(near[block], 0.0, term)
                if block == 0:
                    outer[0, part, rows, :] += low
                    inner[part, 1, rows, :] += high
                else:
                    inner[part, 0, rows, :] += low
                    outer[1, part, rows, :] += high
        return carry

    lax.fori_loop(0, counts[0, 0], one_slot, 0)
    out_a[...] = outer[1 - odd_col]
    out_b[...] = outer[odd_col]


VMEM = pl.BlockSpec(memory_space=pltpu.VMEM)
SMEM = pl.BlockSpec(memory_space=pltpu.SMEM)


def shaped(*dims):
    return jax.ShapeDtypeStruct(dims, jnp.float32)


def whole(body, outs, scalars, arrays, scratch=(), limit=40 << 20, flops=1 << 20):
    return pl.pallas_call(
        body,
        out_shape=outs,
        in_specs=[SMEM] * len(scalars) + [VMEM] * len(arrays),
        out_specs=tuple(VMEM for _ in outs),
        scratch_shapes=scratch,
        compiler_params=pltpu.CompilerParams(vmem_limit_bytes=limit),
        cost_estimate=pl.CostEstimate(flops=flops, bytes_accessed=8 << 20, transcendentals=0),
    )(*scalars, *arrays)


def gradient(info, positions, counts, ext, strip_a, strip_b, measured, rolled, tables):
    extent = ext.shape[2]
    strip = shaped(2, extent, HALF)
    return whole(
        gradient_body,
        (strip, strip, shaped(2, 2, extent, HALF)),
        (info, positions, counts),
        (ext, strip_a, strip_b, measured, rolled, *tables),
        [pltpu.VMEM((2, 2, extent, HALF), jnp.float32)] * 2,
        flops=6 * 8 * 3 * 2**25,
    )


def extend_body(info, tile, halo_a, halo_b, ext, out_a, out_b):
    size = tile.shape[1]
    odd_row, odd_col = info[0], info[1]
    top, bottom = info[2], info[3]
    above = jnp.where(top == 1, 0.0, jnp.where(odd_row == 1, halo_a[0], halo_b[0]))
    below = jnp.where(bottom == 1, 0.0, jnp.where(odd_row == 1, halo_b[1], halo_a[1]))
    for block in range(2):
        cut = slice(block * HALF, (block + 1) * HALF)
        ext[:, block, :MARGIN] = above[:, :, cut]
        ext[:, block, MARGIN : MARGIN + size] = tile[:, :, cut]
        ext[:, block, MARGIN + size :] = below[:, :, cut]
    for part in range(2):
        out_a[part] = ext[part, 1 - odd_col]
        out_b[part] = ext[part, odd_col]


def join_body(width, info, inner, strip_a, strip_b, total, out_a, out_b):
    extent = inner.shape[2]
    odd_row, odd_col = info[0], info[1]
    low = jnp.where(info[4] == 1, 0.0, jnp.where(odd_col == 1, strip_a[0], strip_b[0]))
    high = jnp.where(info[5] == 1, 0.0, jnp.where(odd_col == 1, strip_b[1], strip_a[1]))
    total[:, 0] = inner[:, 0] + low
    total[:, 1] = inner[:, 1] + high
    upper = pl.multiple_of((1 - odd_row) * (extent - width), 8)
    lower = pl.multiple_of(odd_row * (extent - width), 8)
    out_a[...] = total[:, :, pl.ds(upper, width), :]
    out_b[...] = total[:, :, pl.ds(lower, width), :]


def update_body(info, ext, total, halo_a, halo_b, out, out_a, out_b):
    middle = total.shape[2] // 2
    odd_row, odd_col = info[0], info[1]
    top, bottom = info[2], info[3]
    above = jnp.where(top == 1, 0.0, jnp.where(odd_row == 1, halo_a[0], halo_b[0]))
    below = jnp.where(bottom == 1, 0.0, jnp.where(odd_row == 1, halo_b[1], halo_a[1]))
    row = lax.broadcasted_iota(jnp.int32, (1, 1, middle, HALF), 2)
    above = jnp.where((top == 1) & (row < MARGIN), 0.0, total[:, :, :middle] + above)
    below = jnp.where((bottom == 1) & (row >= middle - MARGIN), 0.0, total[:, :, middle:] + below)
    out[:, :, :middle] = ext[:, :, :middle] - step_rate * above
    out[:, :, middle:] = ext[:, :, middle:] - step_rate * below
    for part in range(2):
        out_a[part] = out[part, 1 - odd_col]
        out_b[part] = out[part, odd_col]


def finish_body(info, ext, total, halo_a, halo_b, out):
    size = out.shape[1]
    half = size // 2
    odd_row = info[0]
    above = jnp.where(info[2] == 1, 0.0, jnp.where(odd_row == 1, halo_a[0], halo_b[0]))
    below = jnp.where(info[3] == 1, 0.0, jnp.where(odd_row == 1, halo_b[1], halo_a[1]))
    for block in range(2):
        cut = slice(block * HALF, (block + 1) * HALF)
        upper = slice(MARGIN, MARGIN + half)
        lower = slice(MARGIN + half, MARGIN + size)
        out[:, :half, cut] = ext[:, block, upper] - step_rate * (total[:, block, upper] + above[:, block])
        out[:, half:, cut] = ext[:, block, lower] - step_rate * (total[:, block, lower] + below[:, block])


def constants(size):
    half = size // 2
    mixed, twiddle = rotation_tables(size)
    upper = mixed.astype(jnp.bfloat16)
    lower = (mixed - upper.astype(np.float32)).astype(jnp.bfloat16)
    fore_lane = jnp.asarray(np.concatenate([upper, upper, lower], axis=0))
    back_row = jnp.asarray(np.concatenate([upper, upper, lower], axis=1))
    fore_row = jnp.asarray(np.concatenate([upper.T, upper.T, lower.T], axis=1))
    back_lane = jnp.asarray(np.concatenate([upper.T, upper.T, lower.T], axis=0))
    twist_lane = jnp.asarray(twiddle.reshape(2, 1, half))
    twist_row = jnp.asarray(np.ascontiguousarray(np.broadcast_to(twiddle[:, :, None], (2, half, size))))
    return fore_lane, fore_row, back_row, back_lane, twist_lane, twist_row


def pairs(count, first):
    return [[i, (i + 1) % count] for i in range(first, count, 2)]


def gathered(value_a, value_b, axis):
    count = lax.axis_size(axis)
    return tuple(
        lax.all_gather(value, axis, axis_index_groups=pairs(count, first))
        for first, value in enumerate((value_a, value_b))
    )


def on_device(object_field, probe, positions, counts, intensity):
    size = probe.shape[1]
    tile = object_field.shape[1]
    extent = tile + 2 * MARGIN
    row, col = lax.axis_index("rows"), lax.axis_index("cols")
    n_rows, n_cols = lax.axis_size("rows"), lax.axis_size("cols")
    info = jnp.stack(
        [row % 2, col % 2, row == 0, row == n_rows - 1, col == 0, col == n_cols - 1]
    ).astype(jnp.int32)
    tables = constants(size)
    order = jnp.asarray(split_order(size)).astype(jnp.bfloat16)
    positions, intensity = positions[0, 0], intensity[0, 0]
    strip = shaped(2, extent, HALF)
    block = shaped(2, 2, extent, HALF)

    edge = tile - MARGIN
    edge_a = lax.dynamic_slice_in_dim(object_field, (1 - row % 2) * edge, MARGIN, 1)
    edge_b = lax.dynamic_slice_in_dim(object_field, (row % 2) * edge, MARGIN, 1)
    halos = gathered(edge_a, edge_b, "rows")
    measured, rolled = prepare(positions, intensity, probe, order)
    ext, side_a, side_b = whole(extend_body, (block, strip, strip), (info,), (object_field, *halos))
    sides = gathered(side_a, side_b, "cols")
    side_a, side_b, inner = gradient(info, positions, counts, ext, *sides, measured, rolled, tables)
    sides = gathered(side_a, side_b, "cols")
    width = extent // 2
    part = shaped(2, 2, width, HALF)
    total, edge_a, edge_b = whole(
        functools.partial(join_body, width), (block, part, part), (info,), (inner, *sides)
    )
    halos = gathered(edge_a, edge_b, "rows")
    ext, side_a, side_b = whole(update_body, (block, strip, strip), (info,), (ext, total, *halos))
    sides = gathered(side_a, side_b, "cols")
    side_a, side_b, inner = gradient(info, positions, counts, ext, *sides, measured, rolled, tables)
    sides = gathered(side_a, side_b, "cols")
    part = shaped(2, 2, MARGIN, HALF)
    total, edge_a, edge_b = whole(
        functools.partial(join_body, MARGIN), (block, part, part), (info,), (inner, *sides)
    )
    halos = gathered(edge_a, edge_b, "rows")
    return whole(finish_body, (shaped(2, tile, tile),), (info,), (ext, total, *halos))[0]


def solution(mesh):
    placed = (
        P(None, "rows", "cols"),
        P(),
        P("rows", "cols", None, None),
        P("rows", "cols"),
        P("rows", "cols", None, None, None),
    )
    return jax.shard_map(
        on_device, mesh=mesh, in_specs=placed, out_specs=P(None, "rows", "cols"), check_vma=False
    )
```

profile of v0, /device:TPU:10, one launch (start us, length us, event | category | flops | bytes accessed | tf_op | source)
XLA Modules:
  0.0 303.8 jit_solution(5647118703670805468)
XLA Ops:
  7.7 11.1 %all-gather.1 = f32[4,128,256]{2,1,0:T(8,128)S(1)} all-gather(f32[2,128,256]{2,1,0:T(8,128)S(1)} %get-tuple-element.45), channel_id=3, replica_groups={{16,32},{48,64},{80,96},{112,0},{17,33},{49,65},{81,97},{113,1},{18,34}..., dimensions={0}, use_global_device_ids=true | all-gather | bytes 786432 | tf_op jit(solution)/shard_map/all_gather | solution.py:308
  18.8 9.5 %all-gather = f32[4,128,256]{2,1,0:T(8,128)S(1)} all-gather(f32[2,128,256]{2,1,0:T(8,128)S(1)} %get-tuple-element.46), channel_id=2, replica_groups={{0,16},{32,48},{64,80},{96,112},{1,17},{33,49},{65,81},{97,113},{2,18},..., dimensions={0}, use_global_device_ids=true | all-gather | bytes 786432 | tf_op jit(solution)/shard_map/all_gather | solution.py:308
  28.4 1.7 shard_map.118
  31.7 1.4 copy-done.12
  34.0 5.8 %shard_map.119 = (f32[6,2,128,256]{3,2,1,0:T(8,128)S(1)}, f32[6,2,256,256]{3,2,1,0:T(8,128)S(1)}) custom-call(s32[6,2]{1,0:T(8,128)S(1)} %copy.17.positions, s32[6,256,256]{2,1,0:T(8,128)S(1)} %bitcast.32, f32[2,256,256]{2,1,0:T(8,128)S(1)} %copy-done.17, bf16[256,256]{1,0:T(8,128)(2,1)S(1)} %copy-done.26), custom_call_target="tpu_custom_call" | custom-call | flops 805306368 | bytes 8388608 | tf_op jit(solution)/shard_map/pallas_call | solution.py:65
  39.9 1.6 copy-done.28
  42.6 2.7 all-gather.25.cloned.1.call-done
  45.4 22.6 %all-gather.27.cloned.1.call-done = f32[4,512,128]{2,1,0:T(8,128)} async-done(((f32[2,512,128]{2,1,0:T(8,128)}), f32[4,512,128]{2,1,0:T(8,128)}) %all-gather.27.cloned.1.call-update) | async-done | bytes 1048592 | tf_op jit(solution)/shard_map/all_gather | solution.py:308
  69.2 1.2 copy-done.16
  70.4 1.9 copy-done.29
  72.3 1.4 copy-done.32
  73.7 10.6 %shard_map.120 = (f32[2,512,128]{2,1,0:T(8,128)}, f32[2,512,128]{2,1,0:T(8,128)}, f32[2,2,512,128]{3,2,1,0:T(8,128)S(1)}) custom-call(s32[6]{0:T(128)S(1)} %stack.43.info, s32[6,2]{1,0:T(8,128)S(1)} %copy.17.positions, s32[1,1]{1,0:T(1,128)S(6)} %copy.19.counts, f32[2,2,512,128]{3,2,1,0:T(8,128)S(1)} %get-tuple-element.25.ext, ...), custom_call_target="tpu_custom_call" | custom-call | flops 4831838208 | bytes 8388608 | tf_op jit(solution)/shard_map/pallas_call | solution.py:204
  86.0 12.4 %all-gather.29.cloned.1.call-done = f32[4,512,128]{2,1,0:T(8,128)} async-done(((f32[2,512,128]{2,1,0:T(8,128)}), f32[4,512,128]{2,1,0:T(8,128)}) %all-gather.29.cloned.1.call-update) | async-done | bytes 1048592 | tf_op jit(solution)/shard_map/all_gather | solution.py:308
  98.4 22.4 %all-gather.31.cloned.1.call-done = f32[4,512,128]{2,1,0:T(8,128)} async-done(((f32[2,512,128]{2,1,0:T(8,128)}), f32[4,512,128]{2,1,0:T(8,128)}) %all-gather.31.cloned.1.call-update) | async-done | bytes 1048592 | tf_op jit(solution)/shard_map/all_gather | solution.py:308
  120.8 1.2 copy-done.4
  124.5 2.0 shard_map.121
  127.1 23.5 %all-gather.33.cloned.1.call-done = f32[4,2,256,128]{3,2,1,0:T(8,128)} async-done(((f32[2,2,256,128]{3,2,1,0:T(8,128)}), f32[4,2,256,128]{3,2,1,0:T(8,128)}) %all-gather.33.cloned.1.call-update) | async-done | bytes 1048592 | tf_op jit(solution)/shard_map/all_gather | solution.py:308
  150.6 26.3 %all-gather.35.cloned.1.call-done = f32[4,2,256,128]{3,2,1,0:T(8,128)} async-done(((f32[2,2,256,128]{3,2,1,0:T(8,128)}), f32[4,2,256,128]{3,2,1,0:T(8,128)}) %all-gather.35.cloned.1.call-update) | async-done | bytes 1048592 | tf_op jit(solution)/shard_map/all_gather | solution.py:308
  176.9 1.2 copy-done.1
  178.1 1.2 copy-done.2
  179.3 2.1 shard_map.122
  183.2 12.2 %all-gather.37.cloned.1.call-done = f32[4,512,128]{2,1,0:T(8,128)} async-done(((f32[2,512,128]{2,1,0:T(8,128)}), f32[4,512,128]{2,1,0:T(8,128)}) %all-gather.37.cloned.1.call-update) | async-done | bytes 1048592 | tf_op jit(solution)/shard_map/all_gather | solution.py:308
  195.4 22.6 %all-gather.39.cloned.1.call-done = f32[4,512,128]{2,1,0:T(8,128)} async-done(((f32[2,512,128]{2,1,0:T(8,128)}), f32[4,512,128]{2,1,0:T(8,128)}) %all-gather.39.cloned.1.call-update) | async-done | bytes 1048592 | tf_op jit(solution)/shard_map/all_gather | solution.py:308
  217.9 1.2 copy-done.10
  223.6 1.9 copy-done.30
  225.5 1.4 copy-done.33
  226.9 10.7 %shard_map.123 = (f32[2,512,128]{2,1,0:T(8,128)}, f32[2,512,128]{2,1,0:T(8,128)}, f32[2,2,512,128]{3,2,1,0:T(8,128)S(1)}) custom-call(s32[6]{0:T(128)S(1)} %stack.43.info, s32[6,2]{1,0:T(8,128)S(1)} %copy.17.positions, s32[1,1]{1,0:T(1,128)S(6)} %copy.19.counts, f32[2,2,512,128]{3,2,1,0:T(8,128)S(1)} %copy-done.10, f32[2,2,512,128]{3,2,1,0:T(8,128)S(1)} %bitcast.33, ...), custom_call_target="tpu_custom_call" | custom-call | flops 4831838208 | bytes 8388608 | tf_op jit(solution)/shard_map/pallas_call | solution.py:204
  238.2 12.4 %all-gather.41.cloned.1.call-done = f32[4,512,128]{2,1,0:T(8,128)} async-done(((f32[2,512,128]{2,1,0:T(8,128)}), f32[4,512,128]{2,1,0:T(8,128)}) %all-gather.41.cloned.1.call-update) | async-done | bytes 1048592 | tf_op jit(solution)/shard_map/all_gather | solution.py:308
  250.5 22.4 %all-gather.43.cloned.1.call-done = f32[4,512,128]{2,1,0:T(8,128)} async-done(((f32[2,512,128]{2,1,0:T(8,128)}), f32[4,512,128]{2,1,0:T(8,128)}) %all-gather.43.cloned.1.call-update) | async-done | bytes 1048592 | tf_op jit(solution)/shard_map/all_gather | solution.py:308
  276.3 9.7 %all-gather.12 = f32[4,2,128,128]{3,2,1,0:T(8,128)S(1)} all-gather(f32[2,2,128,128]{3,2,1,0:T(8,128)S(1)} %get-tuple-element.43), channel_id=14, replica_groups={{0,16},{32,48},{64,80},{96,112},{1,17},{33,49},{65,81},{97,113},{2,18},..., dimensions={0}, use_global_device_ids=true | all-gather | bytes 786432 | tf_op jit(solution)/shard_map/all_gather | solution.py:308
  286.0 9.5 %all-gather.13 = f32[4,2,128,128]{3,2,1,0:T(8,128)S(1)} all-gather(f32[2,2,128,128]{3,2,1,0:T(8,128)S(1)} %get-tuple-element.44), channel_id=15, replica_groups={{16,32},{48,64},{80,96},{112,0},{17,33},{49,65},{81,97},{113,1},{18,34}..., dimensions={0}, use_global_device_ids=true | all-gather | bytes 786432 | tf_op jit(solution)/shard_map/all_gather | solution.py:308
  295.5 1.4 shard_map.125
  (83 shorter events, 20.3 us)
Async XLA Ops:
  6.5 21.8 %copy-start = (f32[2,256,256]{2,1,0:T(8,128)S(1)}, f32[2,256,256]{2,1,0:T(8,128)}, u32[]{:S(2)}) copy-start(f32[2,256,256]{2,1,0:T(8,128)} %tile.1) | copy-start | bytes 1572868
  6.5 38.8 %all-gather.25.cloned.1.call-start = ((), (), s32[]{:S(2)}) async-start(), calls=%async_computation | async-start | bytes 1572864 | tf_op jit(solution)/shard_map/all_gather | solution.py:308
  18.8 12.8 %copy-start.34 = (s32[1,1,6,2]{2,3,1,0:T(2,128)S(1)}, s32[1,1,6,2]{2,3,1,0:T(2,128)}, u32[]{:S(2)}) copy-start(s32[1,1,6,2]{2,3,1,0:T(2,128)} %param.14) | copy-start | bytes 148
  18.8 12.9 %copy-start.17 = (f32[2,256,256]{2,1,0:T(8,128)S(1)}, f32[2,256,256]{2,1,0:T(8,128)}, u32[]{:S(2)}) copy-start(f32[2,256,256]{2,1,0:T(8,128)} %probe.1) | copy-start | bytes 1572868
  30.1 37.8 %all-gather.27.cloned.1.call-start = ((), (), s32[]{:S(2)}) async-start(), calls=%async_computation.1 | async-start | bytes 1572864 | tf_op jit(solution)/shard_map/all_gather | solution.py:308
  30.2 37.8 %copy-start.18 = (bf16[768,256]{1,0:T(8,128)(2,1)S(1)}, bf16[768,256]{1,0:T(8,128)(2,1)}, u32[]{:S(2)}) copy-start(bf16[768,256]{1,0:T(8,128)(2,1)} %constant.57.clone.back_lane) | copy-start | bytes 1179652
  30.9 37.1 %copy-start.27 = (f32[2,1,128]{2,1,0:T(1,128)S(1)}, f32[2,1,128]{2,1,0:T(1,128)}, u32[]{:S(2)}) copy-start(f32[2,1,128]{2,1,0:T(1,128)} %constant.58.clone.twist_lane) | copy-start | bytes 3076
  30.9 67.5 %all-gather.29.cloned.1.call-start = ((), (), s32[]{:S(2)}) async-start(), calls=%async_computation.2 | async-start | bytes 1572864 | tf_op jit(solution)/shard_map/all_gather | solution.py:308
  31.7 1.4 copy-start.12
  34.0 34.0 %copy-start.19 = (bf16[256,768]{1,0:T(8,128)(2,1)S(1)}, bf16[256,768]{1,0:T(8,128)(2,1)}, u32[]{:S(2)}) copy-start(bf16[256,768]{1,0:T(8,128)(2,1)} %constant.56.clone.fore_row) | copy-start | bytes 1179652
  34.0 34.0 %copy-start.20 = (bf16[256,768]{1,0:T(8,128)(2,1)S(1)}, bf16[256,768]{1,0:T(8,128)(2,1)}, u32[]{:S(2)}) copy-start(bf16[256,768]{1,0:T(8,128)(2,1)} %constant.55.clone.back_row) | copy-start | bytes 1179652
  34.0 34.0 %copy-start.22 = (bf16[768,256]{1,0:T(8,128)(2,1)S(1)}, bf16[768,256]{1,0:T(8,128)(2,1)}, u32[]{:S(2)}) copy-start(bf16[768,256]{1,0:T(8,128)(2,1)} %constant.54.clone.fore_lane) | copy-start | bytes 1179652
  34.0 34.0 %copy-start.24 = (f32[2,128,256]{2,1,0:T(8,128)S(1)}, f32[2,128,256]{2,1,0:T(8,128)}, u32[]{:S(2)}) copy-start(f32[2,128,256]{2,1,0:T(8,128)} %constant.59.clone.twist_row) | copy-start | bytes 786436
  39.9 1.6 copy-start.28
  68.0 1.2 copy-start.14
  69.2 1.2 copy-start.16
  70.4 1.9 copy-start.29
  72.3 1.4 copy-start.32
  85.4 35.4 %all-gather.31.cloned.1.call-start = ((), (), s32[]{:S(2)}) async-start(), calls=%async_computation.3 | async-start | bytes 1572864 | tf_op jit(solution)/shard_map/all_gather | solution.py:308
  86.0 64.6 %all-gather.33.cloned.1.call-start = ((), (), s32[]{:S(2)}) async-start(), calls=%async_computation.4 | async-start | bytes 1572864 | tf_op jit(solution)/shard_map/all_gather | solution.py:308
  120.8 1.2 copy-start.4
  122.0 1.2 copy-start.5
  126.5 50.4 %all-gather.35.cloned.1.call-start = ((), (), s32[]{:S(2)}) async-start(), calls=%async_computation.5 | async-start | bytes 1572864 | tf_op jit(solution)/shard_map/all_gather | solution.py:308
  127.0 68.3 %all-gather.37.cloned.1.call-start = ((), (), s32[]{:S(2)}) async-start(), calls=%async_computation.6 | async-start | bytes 1572864 | tf_op jit(solution)/shard_map/all_gather | solution.py:308
  179.3 38.6 %copy-start.21 = (bf16[256,768]{1,0:T(8,128)(2,1)S(1)}, bf16[256,768]{1,0:T(8,128)(2,1)}, u32[]{:S(2)}) copy-start(bf16[256,768]{1,0:T(8,128)(2,1)} %constant.55.clone.back_row) | copy-start | bytes 1179652
  182.4 35.5 %all-gather.39.cloned.1.call-start = ((), (), s32[]{:S(2)}) async-start(), calls=%async_computation.7 | async-start | bytes 1572864 | tf_op jit(solution)/shard_map/all_gather | solution.py:308
  183.2 67.4 %all-gather.41.cloned.1.call-start = ((), (), s32[]{:S(2)}) async-start(), calls=%async_computation.8 | async-start | bytes 1572864 | tf_op jit(solution)/shard_map/all_gather | solution.py:308
  217.9 1.2 copy-start.10
  223.6 1.9 copy-start.30
  225.5 1.4 copy-start.33
  237.6 35.4 %all-gather.43.cloned.1.call-start = ((), (), s32[]{:S(2)}) async-start(), calls=%async_computation.9 | async-start | bytes 1572864 | tf_op jit(solution)/shard_map/all_gather | solution.py:308
  276.3 19.3 %copy-start.11 = (f32[2,2,512,128]{3,2,1,0:T(8,128)S(1)}, f32[2,2,512,128]{3,2,1,0:T(8,128)}, u32[]{:S(2)}) copy-start(f32[2,2,512,128]{3,2,1,0:T(8,128)} %copy-done.9) | copy-start | bytes 3145732
  (13 other events, 14.7 us)
Sparse Core Ops, SparseCore 0:
  30.2 15.0 all-gather.24
  47.0 20.8 all-gather.26
  85.5 12.8 all-gather.28
  99.9 20.8 all-gather.30
  126.6 23.9 all-gather.32
  152.1 24.7 all-gather.34
  182.5 12.7 all-gather.36
  197.0 20.8 all-gather.38
  237.7 12.7 all-gather.40
  252.0 20.8 all-gather.42
where the time goes:
time: 306 us; the launch traced here: 304 us
  waiting for transfers between devices  182 us (59%)
  blocking collectives  39.9 us (13%)
  Pallas kernels  35.2 us (12%)
  local copies, waits for them, and re-layouts  31.7 us (10%)
  between operations  14.3 us (5%)
    all_gather x10, waiting for transfers between devices, gathered(): lax.all_gather(value, axis, axis_index_groups=pairs(count, first))  179 us
    all_gather x4, blocking collectives, gathered(): lax.all_gather(value, axis, axis_index_groups=pairs(count, first))  39.9 us
    unnamed x70, local copies, waits for them, and re-layouts  30.4 us
    pallas_call x7, Pallas kernels, whole(): pl.pallas_call(body, out_shape=outs, in_specs=[SMEM] * len(scalars) + [VM...  29.4 us
  transfers between devices with their start and end apart: 10, of which 10 were waited for; matrix products, arithmetic and copies ran while one was open for 0% of the time, Pallas kernels for 2%

commit v1 on v0

--- a/solution.py
+++ b/solution.py
@@ -111,8 +111,8 @@
     lanes = lax.broadcasted_iota(jnp.int32, (1, half), 1)
     inner[...] = jnp.zeros_like(inner)
     outer[...] = jnp.zeros_like(outer)
-    sides[0] = jnp.where(info[4] == 1, 0.0, jnp.where(odd_col == 1, strip_a[0], strip_b[0]))
-    sides[1] = jnp.where(info[5] == 1, 0.0, jnp.where(odd_col == 1, strip_b[1], strip_a[1]))
+    sides[1 - odd_col] = strip_a[...]
+    sides[odd_col] = strip_b[...]
 
     def one_slot(slot, carry):
         srow = positions[slot, 0]
@@ -228,9 +228,8 @@
 def extend_body(info, tile, halo_a, halo_b, ext, out_a, out_b):
     size = tile.shape[1]
     odd_row, odd_col = info[0], info[1]
-    top, bottom = info[2], info[3]
-    above = jnp.where(top == 1, 0.0, jnp.where(odd_row == 1, halo_a[0], halo_b[0]))
-    below = jnp.where(bottom == 1, 0.0, jnp.where(odd_row == 1, halo_b[1], halo_a[1]))
+    above = jnp.where(odd_row == 1, halo_a[...], halo_b[...])
+    below = jnp.where(odd_row == 1, halo_b[...], halo_a[...])
     for block in range(2):
         cut = slice(block * HALF, (block + 1) * HALF)
         ext[:, block, :MARGIN] = above[:, :, cut]
@@ -244,8 +243,8 @@
 def join_body(width, info, inner, strip_a, strip_b, total, out_a, out_b):
     extent = inner.shape[2]
     odd_row, odd_col = info[0], info[1]
-    low = jnp.where(info[4] == 1, 0.0, jnp.where(odd_col == 1, strip_a[0], strip_b[0]))
-    high = jnp.where(info[5] == 1, 0.0, jnp.where(odd_col == 1, strip_b[1], strip_a[1]))
+    low = jnp.where(odd_col == 1, strip_a[...], strip_b[...])
+    high = jnp.where(odd_col == 1, strip_b[...], strip_a[...])
     total[:, 0] = inner[:, 0] + low
     total[:, 1] = inner[:, 1] + high
     upper = pl.multiple_of((1 - odd_row) * (extent - width), 8)
@@ -257,12 +256,11 @@
 def update_body(info, ext, total, halo_a, halo_b, out, out_a, out_b):
     middle = total.shape[2] // 2
     odd_row, odd_col = info[0], info[1]
-    top, bottom = info[2], info[3]
-    above = jnp.where(top == 1, 0.0, jnp.where(odd_row == 1, halo_a[0], halo_b[0]))
-    below = jnp.where(bottom == 1, 0.0, jnp.where(odd_row == 1, halo_b[1], halo_a[1]))
+    above = jnp.where(odd_row == 1, halo_a[...], halo_b[...])
+    below = jnp.where(odd_row == 1, halo_b[...], halo_a[...])
     row = lax.broadcasted_iota(jnp.int32, (1, 1, middle, HALF), 2)
-    above = jnp.where((top == 1) & (row < MARGIN), 0.0, total[:, :, :middle] + above)
-    below = jnp.where((bottom == 1) & (row >= middle - MARGIN), 0.0, total[:, :, middle:] + below)
+    above = jnp.where((info[2] == 1) & (row < MARGIN), 0.0, total[:, :, :middle] + above)
+    below = jnp.where((info[3] == 1) & (row >= middle - MARGIN), 0.0, total[:, :, middle:] + below)
     out[:, :, :middle] = ext[:, :, :middle] - step_rate * above
     out[:, :, middle:] = ext[:, :, middle:] - step_rate * below
     for part in range(2):
@@ -274,8 +272,8 @@
     size = out.shape[1]
     half = size // 2
     odd_row = info[0]
-    above = jnp.where(info[2] == 1, 0.0, jnp.where(odd_row == 1, halo_a[0], halo_b[0]))
-    below = jnp.where(info[3] == 1, 0.0, jnp.where(odd_row == 1, halo_b[1], halo_a[1]))
+    above = jnp.where(odd_row == 1, halo_a[...], halo_b[...])
+    below = jnp.where(odd_row == 1, halo_b[...], halo_a[...])
     for block in range(2):
         cut = slice(block * HALF, (block + 1) * HALF)
         upper = slice(MARGIN, MARGIN + half)
@@ -298,16 +296,28 @@
     return fore_lane, fore_row, back_row, back_lane, twist_lane, twist_row
 
 
-def pairs(count, first):
-    return [[i, (i + 1) % count] for i in range(first, count, 2)]
-
-
-def gathered(value_a, value_b, axis):
+def swapped(value, axis, first):
     count = lax.axis_size(axis)
-    return tuple(
-        lax.all_gather(value, axis, axis_index_groups=pairs(count, first))
-        for first, value in enumerate((value_a, value_b))
-    )
+    route = []
+    for i in range(first, count - 1, 2):
+        route += [(i, i + 1), (i + 1, i)]
+    return lax.ppermute(value, axis, route)
+
+
+def paired(value, axis):
+    groups = [[i, i + 1] for i in range(0, lax.axis_size(axis), 2)]
+    other = 1 - lax.axis_index(axis) % 2
+    parts = []
+    for part in range(value.shape[0]):
+        both = lax.all_gather(value[part], axis, axis_index_groups=groups)
+        parts.append(lax.dynamic_index_in_dim(both, other, 0, keepdims=False))
+    return jnp.stack(parts)
+
+
+def exchanged(value_a, value_b, axis):
+    far = swapped(value_b, axis, 1)
+    near = paired(value_a, axis) if axis == "cols" else swapped(value_a, axis, 0)
+    return near, far
 
 
 def on_device(object_field, probe, positions, counts, intensity):
@@ -315,10 +325,8 @@
     tile = object_field.shape[1]
     extent = tile + 2 * MARGIN
     row, col = lax.axis_index("rows"), lax.axis_index("cols")
-    n_rows, n_cols = lax.axis_size("rows"), lax.axis_size("cols")
-    info = jnp.stack(
-        [row % 2, col % 2, row == 0, row == n_rows - 1, col == 0, col == n_cols - 1]
-    ).astype(jnp.int32)
+    last = lax.axis_size("rows") - 1
+    info = jnp.stack([row % 2, col % 2, row == 0, row == last]).astype(jnp.int32)
     tables = constants(size)
     order = jnp.asarray(split_order(size)).astype(jnp.bfloat16)
     positions, intensity = positions[0, 0], intensity[0, 0]
@@ -328,27 +336,27 @@
     edge = tile - MARGIN
     edge_a = lax.dynamic_slice_in_dim(object_field, (1 - row % 2) * edge, MARGIN, 1)
     edge_b = lax.dynamic_slice_in_dim(object_field, (row % 2) * edge, MARGIN, 1)
-    halos = gathered(edge_a, edge_b, "rows")
+    halos = exchanged(edge_a, edge_b, "rows")
     measured, rolled = prepare(positions, intensity, probe, order)
     ext, side_a, side_b = whole(extend_body, (block, strip, strip), (info,), (object_field, *halos))
-    sides = gathered(side_a, side_b, "cols")
+    sides = exchanged(side_a, side_b, "cols")
     side_a, side_b, inner = gradient(info, positions, counts, ext, *sides, measured, rolled, tables)
-    sides = gathered(side_a, side_b, "cols")
+    sides = exchanged(side_a, side_b, "cols")
     width = extent // 2
     part = shaped(2, 2, width, HALF)
     total, edge_a, edge_b = whole(
         functools.partial(join_body, width), (block, part, part), (info,), (inner, *sides)
     )
-    halos = gathered(edge_a, edge_b, "rows")
+    halos = exchanged(edge_a, edge_b, "rows")
     ext, side_a, side_b = whole(update_body, (block, strip, strip), (info,), (ext, total, *halos))
-    sides = gathered(side_a, side_b, "cols")
+    sides = exchanged(side_a, side_b, "cols")
     side_a, side_b, inner = gradient(info, positions, counts, ext, *sides, measured, rolled, tables)
-    sides = gathered(side_a, side_b, "cols")
+    sides = exchanged(side_a, side_b, "cols")
     part = shaped(2, 2, MARGIN, HALF)
     total, edge_a, edge_b = whole(
         functools.partial(join_body, MARGIN), (block, part, part), (info,), (inner, *sides)
     )
-    halos = gathered(edge_a, edge_b, "rows")
+    halos = exchanged(edge_a, edge_b, "rows")
     return whole(finish_body, (shaped(2, tile, tile),), (info,), (ext, total, *halos))[0]
 
 

time: 306 us -> 133 us (0.43)
  waiting for transfers between devices: 182 us -> 47.2 us
  starting transfers between devices: 0.36 us -> 33.7 us
  local copies, waits for them, and re-layouts: 31.7 us -> 5.52 us
  blocking collectives: 39.9 us -> 18.5 us
  between operations: 14.3 us -> 0.91 us
  Pallas kernels: 35.2 us -> 26.2 us
    all_gather x10 -> x0, waiting for transfers between devices: 179 us -> none  [gathered(): lax.all_gather(value, axis, axis_index_groups=pairs(count, first))]
    ppermute x0 -> x10, waiting for transfers between devices: none -> 47.2 us  [swapped(): return lax.ppermute(value, axis, route)]
    ppermute x0 -> x10, starting transfers between devices: none -> 33.7 us  [swapped(): return lax.ppermute(value, axis, route)]
    unnamed x70 -> x20, local copies, waits for them, and re-layouts: 30.4 us -> 3.39 us
    all_gather x4 -> x8, blocking collectives: 39.9 us -> 18.5 us  [paired(): both = lax.all_gather(value[part], axis, axis_index_groups=groups)]
    pallas_call x7, Pallas kernels: 29.4 us -> 20.4 us  [whole(): pl.pallas_call(body, out_shape=outs, in_specs=[SMEM] * len(scalars) + [VM...]
  transfers between devices with their start and end apart: 10 -> 10, of which waited for: 10 -> 9; matrix products, arithmetic and copies ran while one was open for 0% -> 1% of each run, Pallas kernels for 2% -> 4%
where the time goes in v1:
time: 133 us; the launch traced here: 132 us
  waiting for transfers between devices  47.2 us (35%)
  starting transfers between devices  33.7 us (25%)
  Pallas kernels  26.2 us (20%)
  blocking collectives  18.5 us (14%)
  local copies, waits for them, and re-layouts  5.52 us (4%)
    ppermute x10, waiting for transfers between devices, swapped(): return lax.ppermute(value, axis, route)  47.2 us
    ppermute x10, starting transfers between devices, swapped(): return lax.ppermute(value, axis, route)  33.7 us
    pallas_call x7, Pallas kernels, whole(): pl.pallas_call(body, out_shape=outs, in_specs=[SMEM] * len(scalars) + [VM...  20.4 us
    all_gather x8, blocking collectives, paired(): both = lax.all_gather(value[part], axis, axis_index_groups=groups)  18.5 us
    pallas_call x1, Pallas kernels, prepare(): pl.pallas_call(prepare_body, out_shape=(jax.ShapeDtypeStruct((slots, 2, s...  5.82 us
    unnamed x20, local copies, waits for them, and re-layouts  3.39 us
  transfers between devices with their start and end apart: 10, of which 9 were waited for; matrix products, arithmetic and copies ran while one was open for 1% of the time, Pallas kernels for 4%

profile of v1, /device:TPU:10, one launch (start us, length us, event | category | flops | bytes accessed | tf_op | source)
XLA Modules:
  0.0 132.2 jit_solution(4386041150195156690)
XLA Ops:
  0.0 1.1 constant_dynamic-slice_fusion.8
  1.1 4.1 %collective-permute-start.1 = (f32[2,128,256]{2,1,0:T(8,128)S(1)}, f32[2,128,256]{2,1,0:T(8,128)S(1)}, u32[]{:S(2)}, u32[]{:S(2)}) collective-permute-start(f32[2,128,256]{2,1,0:T(8,128)S(1)} %get-tuple-element.53), channel_id=1, source_target_pairs={{16,32},{32,16},{48,64},{64,48},{80,96},{96,80},{17,33},{33,17},{4... | collective-permute-start | bytes 786440 | tf_op jit(solution)/shard_map/ppermute | solution.py:304
  5.1 2.6 %collective-permute-start = (f32[2,128,256]{2,1,0:T(8,128)S(1)}, f32[2,128,256]{2,1,0:T(8,128)S(1)}, u32[]{:S(2)}, u32[]{:S(2)}) collective-permute-start(f32[2,128,256]{2,1,0:T(8,128)S(1)} %get-tuple-element.54), channel_id=1, source_target_pairs={{0,16},{16,0},{32,48},{48,32},{64,80},{80,64},{96,112},{112,96},{1... | collective-permute-start | bytes 786440 | tf_op jit(solution)/shard_map/ppermute | solution.py:304
  9.2 1.4 %copy-done.1 = s32[1,1,6,256,256]{4,3,2,1,0:T(8,128)S(1)} copy-done((s32[1,1,6,256,256]{4,3,2,1,0:T(8,128)S(1)}, s32[1,1,6,256,256]{4,3,2,1,0:T(8,128)}, u32[]{:S(2)}) %copy-start.1) | copy-done | bytes 1572888
  10.6 1.0 copy-done.2
  12.5 5.8 %shard_map.119 = (f32[6,2,128,256]{3,2,1,0:T(8,128)S(1)}, f32[6,2,256,256]{3,2,1,0:T(8,128)S(1)}) custom-call(s32[6,2]{1,0:T(8,128)S(1)} %copy.17.positions, s32[6,256,256]{2,1,0:T(8,128)S(1)} %bitcast.6, f32[2,256,256]{2,1,0:T(8,128)S(1)} %copy-done.2, bf16[256,256]{1,0:T(8,128)(2,1)S(1)} %copy-done.8), custom_call_target="tpu_custom_call" | custom-call | flops 805306368 | bytes 8388608 | tf_op jit(solution)/shard_map/pallas_call | solution.py:65
  20.0 4.5 %collective-permute-start.2 = (f32[2,512,128]{2,1,0:T(8,128)S(1)}, f32[2,512,128]{2,1,0:T(8,128)S(1)}, u32[]{:S(2)}, u32[]{:S(2)}) collective-permute-start(f32[2,512,128]{2,1,0:T(8,128)S(1)} %get-tuple-element.27), channel_id=1, source_target_pairs={{1,2},{2,1},{3,4},{4,3},{5,6},{6,5},{7,8},{8,7},{9,10},{10,9},{11,... | collective-permute-start | bytes 1572872 | tf_op jit(solution)/shard_map/ppermute | solution.py:304
  24.5 2.2 %all_gather.24 = f32[2,512,128]{2,1,0:T(8,128)S(1)} all-gather(f32[1,512,128]{2,1,0:T(8,128)S(1)} %get-tuple-element.51), channel_id=1, replica_groups={{0,1},{2,3},{4,5},{6,7},{8,9},{10,11},{12,13},{14,15},{16,17},{18,19},{..., dimensions={0}, use_global_device_ids=true | all-gather | bytes 786432 | tf_op jit(solution)/shard_map/all_gather | solution.py:312
  26.8 2.3 %all_gather.25 = f32[2,512,128]{2,1,0:T(8,128)S(1)} all-gather(f32[1,512,128]{2,1,0:T(8,128)S(1)} %get-tuple-element.52), channel_id=1, replica_groups={{0,1},{2,3},{4,5},{6,7},{8,9},{10,11},{12,13},{14,15},{16,17},{18,19},{..., dimensions={0}, use_global_device_ids=true | all-gather | bytes 786432 | tf_op jit(solution)/shard_map/all_gather | solution.py:312
  29.2 3.5 %collective-permute-done.2.strip_b = f32[2,512,128]{2,1,0:T(8,128)S(1)} collective-permute-done((f32[2,512,128]{2,1,0:T(8,128)S(1)}, f32[2,512,128]{2,1,0:T(8,128)S(1)}, u32[]{:S(2)}, u32[]{:S(2)}) %collective-permute-start.2) | collective-permute-done | bytes 524320 | tf_op jit(solution)/shard_map/ppermute | solution.py:304
  32.7 7.8 %shard_map.120 = (f32[2,512,128]{2,1,0:T(8,128)S(1)}, f32[2,512,128]{2,1,0:T(8,128)S(1)}, f32[2,2,512,128]{3,2,1,0:T(8,128)S(1)}) custom-call(s32[4]{0:T(128)S(1)} %pad_add_fusion.info, s32[6,2]{1,0:T(8,128)S(1)} %copy.17.positions, s32[1,1]{1,0:T(1,128)S(6)} %copy.19.counts, f32[2,2,512,128]{3,2,1,0:T(8,128)S(1)} %get-tuple-element.25.ext, ...), custom_call_target="tpu_custom_call" | custom-call | flops 4831838208 | bytes 8388608 | tf_op jit(solution)/shard_map/pallas_call | solution.py:204
  40.5 4.5 %collective-permute-start.3 = (f32[2,512,128]{2,1,0:T(8,128)S(1)}, f32[2,512,128]{2,1,0:T(8,128)S(1)}, u32[]{:S(2)}, u32[]{:S(2)}) collective-permute-start(f32[2,512,128]{2,1,0:T(8,128)S(1)} %get-tuple-element.32), channel_id=1, source_target_pairs={{1,2},{2,1},{3,4},{4,3},{5,6},{6,5},{7,8},{8,7},{9,10},{10,9},{11,... | collective-permute-start | bytes 1572872 | tf_op jit(solution)/shard_map/ppermute | solution.py:304
  45.0 2.2 %all_gather.26 = f32[2,512,128]{2,1,0:T(8,128)S(1)} all-gather(f32[1,512,128]{2,1,0:T(8,128)S(1)} %get-tuple-element.49), channel_id=1, replica_groups={{0,1},{2,3},{4,5},{6,7},{8,9},{10,11},{12,13},{14,15},{16,17},{18,19},{..., dimensions={0}, use_global_device_ids=true | all-gather | bytes 786432 | tf_op jit(solution)/shard_map/all_gather | solution.py:312
  47.2 2.2 %all_gather.27 = f32[2,512,128]{2,1,0:T(8,128)S(1)} all-gather(f32[1,512,128]{2,1,0:T(8,128)S(1)} %get-tuple-element.50), channel_id=1, replica_groups={{0,1},{2,3},{4,5},{6,7},{8,9},{10,11},{12,13},{14,15},{16,17},{18,19},{..., dimensions={0}, use_global_device_ids=true | all-gather | bytes 786432 | tf_op jit(solution)/shard_map/all_gather | solution.py:312
  49.5 3.6 %collective-permute-done.3.strip_b = f32[2,512,128]{2,1,0:T(8,128)S(1)} collective-permute-done((f32[2,512,128]{2,1,0:T(8,128)S(1)}, f32[2,512,128]{2,1,0:T(8,128)S(1)}, u32[]{:S(2)}, u32[]{:S(2)}) %collective-permute-start.3) | collective-permute-done | bytes 524320 | tf_op jit(solution)/shard_map/ppermute | solution.py:304
  54.1 4.7 %collective-permute-start.5 = (f32[2,2,256,128]{3,2,1,0:T(8,128)S(1)}, f32[2,2,256,128]{3,2,1,0:T(8,128)S(1)}, u32[]{:S(2)}, u32[]{:S(2)}) collective-permute-start(f32[2,2,256,128]{3,2,1,0:T(8,128)S(1)} %get-tuple-element.35), channel_id=1, source_target_pairs={{16,32},{32,16},{48,64},{64,48},{80,96},{96,80},{17,33},{33,17},{4... | collective-permute-start | bytes 1572872 | tf_op jit(solution)/shard_map/ppermute | solution.py:304
  58.9 11.6 %collective-permute-done.4.halo_a = f32[2,2,256,128]{3,2,1,0:T(8,128)S(1)} collective-permute-done((f32[2,2,256,128]{3,2,1,0:T(8,128)S(1)}, f32[2,2,256,128]{3,2,1,0:T(8,128)S(1)}, u32[]{:S(2)}, u32[]{:S(2)}) %collective-permute-start.4) | collective-permute-done | bytes 524320 | tf_op jit(solution)/shard_map/ppermute | solution.py:304
  70.4 9.6 %collective-permute-done.5.halo_b = f32[2,2,256,128]{3,2,1,0:T(8,128)S(1)} collective-permute-done((f32[2,2,256,128]{3,2,1,0:T(8,128)S(1)}, f32[2,2,256,128]{3,2,1,0:T(8,128)S(1)}, u32[]{:S(2)}, u32[]{:S(2)}) %collective-permute-start.5) | collective-permute-done | bytes 524320 | tf_op jit(solution)/shard_map/ppermute | solution.py:304
  81.1 2.7 %collective-permute-start.6 = (f32[2,512,128]{2,1,0:T(8,128)S(1)}, f32[2,512,128]{2,1,0:T(8,128)S(1)}, u32[]{:S(2)}, u32[]{:S(2)}) collective-permute-start(f32[2,512,128]{2,1,0:T(8,128)S(1)} %get-tuple-element.38), channel_id=1, source_target_pairs={{1,2},{2,1},{3,4},{4,3},{5,6},{6,5},{7,8},{8,7},{9,10},{10,9},{11,... | collective-permute-start | bytes 1572872 | tf_op jit(solution)/shard_map/ppermute | solution.py:304
  83.8 3.1 %all_gather.28 = f32[2,512,128]{2,1,0:T(8,128)S(1)} all-gather(f32[1,512,128]{2,1,0:T(8,128)S(1)} %get-tuple-element.47), channel_id=1, replica_groups={{0,1},{2,3},{4,5},{6,7},{8,9},{10,11},{12,13},{14,15},{16,17},{18,19},{..., dimensions={0}, use_global_device_ids=true | all-gather | bytes 786432 | tf_op jit(solution)/shard_map/all_gather | solution.py:312
  86.9 2.2 %all_gather.29 = f32[2,512,128]{2,1,0:T(8,128)S(1)} all-gather(f32[1,512,128]{2,1,0:T(8,128)S(1)} %get-tuple-element.48), channel_id=1, replica_groups={{0,1},{2,3},{4,5},{6,7},{8,9},{10,11},{12,13},{14,15},{16,17},{18,19},{..., dimensions={0}, use_global_device_ids=true | all-gather | bytes 786432 | tf_op jit(solution)/shard_map/all_gather | solution.py:312
  89.1 4.6 %collective-permute-done.6.strip_b = f32[2,512,128]{2,1,0:T(8,128)S(1)} collective-permute-done((f32[2,512,128]{2,1,0:T(8,128)S(1)}, f32[2,512,128]{2,1,0:T(8,128)S(1)}, u32[]{:S(2)}, u32[]{:S(2)}) %collective-permute-start.6) | collective-permute-done | bytes 524320 | tf_op jit(solution)/shard_map/ppermute | solution.py:304
  93.7 7.7 %shard_map.123 = (f32[2,512,128]{2,1,0:T(8,128)S(1)}, f32[2,512,128]{2,1,0:T(8,128)S(1)}, f32[2,2,512,128]{3,2,1,0:T(8,128)S(1)}) custom-call(s32[4]{0:T(128)S(1)} %pad_add_fusion.info, s32[6,2]{1,0:T(8,128)S(1)} %copy.17.positions, s32[1,1]{1,0:T(1,128)S(6)} %copy.19.counts, f32[2,2,512,128]{3,2,1,0:T(8,128)S(1)} %get-tuple-element.36.ext, ...), custom_call_target="tpu_custom_call" | custom-call | flops 4831838208 | bytes 8388608 | tf_op jit(solution)/shard_map/pallas_call | solution.py:204
  101.5 2.7 %collective-permute-start.7 = (f32[2,512,128]{2,1,0:T(8,128)S(1)}, f32[2,512,128]{2,1,0:T(8,128)S(1)}, u32[]{:S(2)}, u32[]{:S(2)}) collective-permute-start(f32[2,512,128]{2,1,0:T(8,128)S(1)} %get-tuple-element.41), channel_id=1, source_target_pairs={{1,2},{2,1},{3,4},{4,3},{5,6},{6,5},{7,8},{8,7},{9,10},{10,9},{11,... | collective-permute-start | bytes 1572872 | tf_op jit(solution)/shard_map/ppermute | solution.py:304
  104.2 2.2 %all_gather.30 = f32[2,512,128]{2,1,0:T(8,128)S(1)} all-gather(f32[1,512,128]{2,1,0:T(8,128)S(1)} %get-tuple-element.45), channel_id=1, replica_groups={{0,1},{2,3},{4,5},{6,7},{8,9},{10,11},{12,13},{14,15},{16,17},{18,19},{..., dimensions={0}, use_global_device_ids=true | all-gather | bytes 786432 | tf_op jit(solution)/shard_map/all_gather | solution.py:312
  106.4 2.2 %all_gather.31 = f32[2,512,128]{2,1,0:T(8,128)S(1)} all-gather(f32[1,512,128]{2,1,0:T(8,128)S(1)} %get-tuple-element.46), channel_id=1, replica_groups={{0,1},{2,3},{4,5},{6,7},{8,9},{10,11},{12,13},{14,15},{16,17},{18,19},{..., dimensions={0}, use_global_device_ids=true | all-gather | bytes 786432 | tf_op jit(solution)/shard_map/all_gather | solution.py:312
  108.7 5.4 %collective-permute-done.7.strip_b = f32[2,512,128]{2,1,0:T(8,128)S(1)} collective-permute-done((f32[2,512,128]{2,1,0:T(8,128)S(1)}, f32[2,512,128]{2,1,0:T(8,128)S(1)}, u32[]{:S(2)}, u32[]{:S(2)}) %collective-permute-start.7) | collective-permute-done | bytes 524320 | tf_op jit(solution)/shard_map/ppermute | solution.py:304
  114.9 2.8 %collective-permute-start.8 = (f32[2,2,128,128]{3,2,1,0:T(8,128)S(1)}, f32[2,2,128,128]{3,2,1,0:T(8,128)S(1)}, u32[]{:S(2)}, u32[]{:S(2)}) collective-permute-start(f32[2,2,128,128]{3,2,1,0:T(8,128)S(1)} %get-tuple-element.43), channel_id=1, source_target_pairs={{0,16},{16,0},{32,48},{48,32},{64,80},{80,64},{96,112},{112,96},{1... | collective-permute-start | bytes 786440 | tf_op jit(solution)/shard_map/ppermute | solution.py:304
  117.8 4.9 %collective-permute-start.9 = (f32[2,2,128,128]{3,2,1,0:T(8,128)S(1)}, f32[2,2,128,128]{3,2,1,0:T(8,128)S(1)}, u32[]{:S(2)}, u32[]{:S(2)}) collective-permute-start(f32[2,2,128,128]{3,2,1,0:T(8,128)S(1)} %get-tuple-element.44), channel_id=1, source_target_pairs={{16,32},{32,16},{48,64},{64,48},{80,96},{96,80},{17,33},{33,17},{4... | collective-permute-start | bytes 786440 | tf_op jit(solution)/shard_map/ppermute | solution.py:304
  122.6 2.5 %collective-permute-done.8.halo_a = f32[2,2,128,128]{3,2,1,0:T(8,128)S(1)} collective-permute-done((f32[2,2,128,128]{3,2,1,0:T(8,128)S(1)}, f32[2,2,128,128]{3,2,1,0:T(8,128)S(1)}, u32[]{:S(2)}, u32[]{:S(2)}) %collective-permute-start.8) | collective-permute-done | bytes 262176 | tf_op jit(solution)/shard_map/ppermute | solution.py:304
  125.1 5.6 %collective-permute-done.9.halo_b = f32[2,2,128,128]{3,2,1,0:T(8,128)S(1)} collective-permute-done((f32[2,2,128,128]{3,2,1,0:T(8,128)S(1)}, f32[2,2,128,128]{3,2,1,0:T(8,128)S(1)}, u32[]{:S(2)}, u32[]{:S(2)}) %collective-permute-start.9) | collective-permute-done | bytes 262176 | tf_op jit(solution)/shard_map/ppermute | solution.py:304
  130.7 1.5 %shard_map.125 = f32[2,256,256]{2,1,0:T(8,128)} custom-call(s32[4]{0:T(128)S(1)} %pad_add_fusion.info, f32[2,2,512,128]{3,2,1,0:T(8,128)S(1)} %get-tuple-element.36.ext, f32[2,2,512,128]{3,2,1,0:T(8,128)S(1)} %get-tuple-element.42.total, f32[2,2,128,128]{3,2,1,0:T(8,128)S(1)} %collective-permute-done.8.halo_a, ...), custom_call_target="tpu_custom_call" | custom-call | flops 1048576 | bytes 8388608 | tf_op jit(solution)/shard_map/pallas_call | solution.py:204
  (43 shorter events, 6.6 us)
Async XLA Ops:
  1.1 18.2 %copy-start = (f32[2,256,256]{2,1,0:T(8,128)S(1)}, f32[2,256,256]{2,1,0:T(8,128)}, u32[]{:S(2)}) copy-start(f32[2,256,256]{2,1,0:T(8,128)} %tile.1) | copy-start | bytes 1572868
  1.1 17.3 %collective-permute-start.1 = (f32[2,128,256]{2,1,0:T(8,128)S(1)}, f32[2,128,256]{2,1,0:T(8,128)S(1)}, u32[]{:S(2)}, u32[]{:S(2)}) collective-permute-start(f32[2,128,256]{2,1,0:T(8,128)S(1)} %get-tuple-element.53), channel_id=1, source_target_pairs={{16,32},{32,16},{48,64},{64,48},{80,96},{96,80},{17,33},{33,17},{4... | collective-permute-start | bytes 786440 | tf_op jit(solution)/shard_map/ppermute | solution.py:304
  5.1 14.1 %collective-permute-start = (f32[2,128,256]{2,1,0:T(8,128)S(1)}, f32[2,128,256]{2,1,0:T(8,128)S(1)}, u32[]{:S(2)}, u32[]{:S(2)}) collective-permute-start(f32[2,128,256]{2,1,0:T(8,128)S(1)} %get-tuple-element.54), channel_id=1, source_target_pairs={{0,16},{16,0},{32,48},{48,32},{64,80},{80,64},{96,112},{112,96},{1... | collective-permute-start | bytes 786440 | tf_op jit(solution)/shard_map/ppermute | solution.py:304
  9.2 1.4 %copy-start.1 = (s32[1,1,6,256,256]{4,3,2,1,0:T(8,128)S(1)}, s32[1,1,6,256,256]{4,3,2,1,0:T(8,128)}, u32[]{:S(2)}) copy-start(s32[1,1,6,256,256]{4,3,2,1,0:T(8,128)} %param.16) | copy-start | bytes 4718596
  10.6 1.0 copy-start.2
  11.6 0.9 copy-start.8
  20.0 12.6 %collective-permute-start.2 = (f32[2,512,128]{2,1,0:T(8,128)S(1)}, f32[2,512,128]{2,1,0:T(8,128)S(1)}, u32[]{:S(2)}, u32[]{:S(2)}) collective-permute-start(f32[2,512,128]{2,1,0:T(8,128)S(1)} %get-tuple-element.27), channel_id=1, source_target_pairs={{1,2},{2,1},{3,4},{4,3},{5,6},{6,5},{7,8},{8,7},{9,10},{10,9},{11,... | collective-permute-start | bytes 1572872 | tf_op jit(solution)/shard_map/ppermute | solution.py:304
  26.7 5.9 %copy-start.3 = (bf16[768,256]{1,0:T(8,128)(2,1)S(1)}, bf16[768,256]{1,0:T(8,128)(2,1)}, u32[]{:S(2)}) copy-start(bf16[768,256]{1,0:T(8,128)(2,1)} %constant.83.clone.back_lane) | copy-start | bytes 1179652
  26.7 5.9 %copy-start.4 = (bf16[256,768]{1,0:T(8,128)(2,1)S(1)}, bf16[256,768]{1,0:T(8,128)(2,1)}, u32[]{:S(2)}) copy-start(bf16[256,768]{1,0:T(8,128)(2,1)} %constant.82.clone.fore_row) | copy-start | bytes 1179652
  26.7 5.9 %copy-start.5 = (bf16[256,768]{1,0:T(8,128)(2,1)S(1)}, bf16[256,768]{1,0:T(8,128)(2,1)}, u32[]{:S(2)}) copy-start(bf16[256,768]{1,0:T(8,128)(2,1)} %constant.81.clone.back_row) | copy-start | bytes 1179652
  26.7 5.9 %copy-start.6 = (bf16[768,256]{1,0:T(8,128)(2,1)S(1)}, bf16[768,256]{1,0:T(8,128)(2,1)}, u32[]{:S(2)}) copy-start(bf16[768,256]{1,0:T(8,128)(2,1)} %constant.80.clone.fore_lane) | copy-start | bytes 1179652
  26.7 5.9 %copy-start.7 = (f32[2,128,256]{2,1,0:T(8,128)S(1)}, f32[2,128,256]{2,1,0:T(8,128)}, u32[]{:S(2)}) copy-start(f32[2,128,256]{2,1,0:T(8,128)} %constant.85.clone.twist_row) | copy-start | bytes 786436
  26.7 5.9 %copy-start.9 = (f32[2,1,128]{2,1,0:T(1,128)S(1)}, f32[2,1,128]{2,1,0:T(1,128)}, u32[]{:S(2)}) copy-start(f32[2,1,128]{2,1,0:T(1,128)} %constant.84.clone.twist_lane) | copy-start | bytes 3076
  40.5 12.6 %collective-permute-start.3 = (f32[2,512,128]{2,1,0:T(8,128)S(1)}, f32[2,512,128]{2,1,0:T(8,128)S(1)}, u32[]{:S(2)}, u32[]{:S(2)}) collective-permute-start(f32[2,512,128]{2,1,0:T(8,128)S(1)} %get-tuple-element.32), channel_id=1, source_target_pairs={{1,2},{2,1},{3,4},{4,3},{5,6},{6,5},{7,8},{8,7},{9,10},{10,9},{11,... | collective-permute-start | bytes 1572872 | tf_op jit(solution)/shard_map/ppermute | solution.py:304
  54.0 16.4 %collective-permute-start.4 = (f32[2,2,256,128]{3,2,1,0:T(8,128)S(1)}, f32[2,2,256,128]{3,2,1,0:T(8,128)S(1)}, u32[]{:S(2)}, u32[]{:S(2)}) collective-permute-start(f32[2,2,256,128]{3,2,1,0:T(8,128)S(1)} %get-tuple-element.34), channel_id=1, source_target_pairs={{0,16},{16,0},{32,48},{48,32},{64,80},{80,64},{96,112},{112,96},{1... | collective-permute-start | bytes 1572872 | tf_op jit(solution)/shard_map/ppermute | solution.py:304
  54.1 25.9 %collective-permute-start.5 = (f32[2,2,256,128]{3,2,1,0:T(8,128)S(1)}, f32[2,2,256,128]{3,2,1,0:T(8,128)S(1)}, u32[]{:S(2)}, u32[]{:S(2)}) collective-permute-start(f32[2,2,256,128]{3,2,1,0:T(8,128)S(1)} %get-tuple-element.35), channel_id=1, source_target_pairs={{16,32},{32,16},{48,64},{64,48},{80,96},{96,80},{17,33},{33,17},{4... | collective-permute-start | bytes 1572872 | tf_op jit(solution)/shard_map/ppermute | solution.py:304
  81.1 12.6 %collective-permute-start.6 = (f32[2,512,128]{2,1,0:T(8,128)S(1)}, f32[2,512,128]{2,1,0:T(8,128)S(1)}, u32[]{:S(2)}, u32[]{:S(2)}) collective-permute-start(f32[2,512,128]{2,1,0:T(8,128)S(1)} %get-tuple-element.38), channel_id=1, source_target_pairs={{1,2},{2,1},{3,4},{4,3},{5,6},{6,5},{7,8},{8,7},{9,10},{10,9},{11,... | collective-permute-start | bytes 1572872 | tf_op jit(solution)/shard_map/ppermute | solution.py:304
  101.5 12.6 %collective-permute-start.7 = (f32[2,512,128]{2,1,0:T(8,128)S(1)}, f32[2,512,128]{2,1,0:T(8,128)S(1)}, u32[]{:S(2)}, u32[]{:S(2)}) collective-permute-start(f32[2,512,128]{2,1,0:T(8,128)S(1)} %get-tuple-element.41), channel_id=1, source_target_pairs={{1,2},{2,1},{3,4},{4,3},{5,6},{6,5},{7,8},{8,7},{9,10},{10,9},{11,... | collective-permute-start | bytes 1572872 | tf_op jit(solution)/shard_map/ppermute | solution.py:304
  114.9 10.2 %collective-permute-start.8 = (f32[2,2,128,128]{3,2,1,0:T(8,128)S(1)}, f32[2,2,128,128]{3,2,1,0:T(8,128)S(1)}, u32[]{:S(2)}, u32[]{:S(2)}) collective-permute-start(f32[2,2,128,128]{3,2,1,0:T(8,128)S(1)} %get-tuple-element.43), channel_id=1, source_target_pairs={{0,16},{16,0},{32,48},{48,32},{64,80},{80,64},{96,112},{112,96},{1... | collective-permute-start | bytes 786440 | tf_op jit(solution)/shard_map/ppermute | solution.py:304
  117.8 12.9 %collective-permute-start.9 = (f32[2,2,128,128]{3,2,1,0:T(8,128)S(1)}, f32[2,2,128,128]{3,2,1,0:T(8,128)S(1)}, u32[]{:S(2)}, u32[]{:S(2)}) collective-permute-start(f32[2,2,128,128]{3,2,1,0:T(8,128)S(1)} %get-tuple-element.44), channel_id=1, source_target_pairs={{16,32},{32,16},{48,64},{64,48},{80,96},{96,80},{17,33},{33,17},{4... | collective-permute-start | bytes 786440 | tf_op jit(solution)/shard_map/ppermute | solution.py:304
